TPU v7x, 256 devices: a whole 4x4x8 slice. The times are simulated.
256 devices in a mesh: frame: 64 (over y, z, core), text: 4 (over x).
Axes of the slice: x: 4, y: 4, z: 8, core: 2. Of those that a mesh axis runs over, the one named last changes fastest.
Arguments:
- frame_keys: bfloat16 [32768, 4096], P('frame', 'text'), may hold values from -6 to 6
- frame_values: bfloat16 [32768, 4096], P('frame', 'text'), may hold values from -6 to 6
- frame_grads: bfloat16 [32768, 4096], P('frame', 'text'), may hold values from -6 to 6
- text_keys: bfloat16 [8192, 4096], P(('frame', 'text')), may hold values from -6 to 6
- text_values: bfloat16 [8192, 4096], P(('frame', 'text')), may hold values from -6 to 6
- text_grads: bfloat16 [8192, 4096], P(('frame', 'text')), may hold values from -6 to 6
- band_first: int32 [256], P('frame'), may hold values from 0 to 63, as said below
- band_count: int32 [256], P('frame'), may hold values from 1 to 3
Outputs:
- frame_out: bfloat16 [32768, 4096], P('frame', 'text')
- text_out: bfloat16 [8192, 4096], P('frame', 'text')
- frame_key_grad: bfloat16 [32768, 4096], P('frame', 'text')
- frame_value_grad: bfloat16 [32768, 4096], P('frame', 'text')
- text_key_grad: bfloat16 [8192, 4096], P('frame', 'text')
- text_value_grad: bfloat16 [8192, 4096], P('frame', 'text')
Inputs may be any that keep to these rules, and one draw needn't show every extreme that they name: For frame block b, band_first[b] is b // 4 - 1 or b // 4, and band_first[b] + band_count[b] - 1 is b // 4 or b // 4 + 1, so every text block lies in some band.
All inputs are finite; a program needn't handle non-finite values.
Results may differ from a plain program's by a relative error of at most 0.023.
Values may be sent and summed in bfloat16 or wider, within the bound.
A program may use at most 128 MiB of HBM per device.

v0:
```python
import functools
import math

import jax
import jax.numpy as jnp
from jax import lax
from jax.experimental import pallas as pl
from jax.experimental.pallas import tpu as pltpu
from jax.sharding import PartitionSpec as P

D = 128
BLOCK = 128
NEGATIVE = -1e30
FLOOR = -1e20
LAG = 2
AHEAD = 4
MESH = pl.DeviceIdType.MESH
F32 = jnp.float32
BF16 = jnp.bfloat16


def dot_nt(a, b):
    return lax.dot_general(a, b, (((1,), (1,)), ((), ())), preferred_element_type=F32)


def dot_nn(a, b):
    return lax.dot_general(a, b, (((1,), (0,)), ((), ())), preferred_element_type=F32)


def dot_tn(a, b):
    return lax.dot_general(a, b, (((0,), (0,)), ((), ())), preferred_element_type=F32)


def kernel(
    fdim, tdim, heads,
    fk_hbm, fv_hbm, fg_hbm, tk_hbm, tv_hbm, tg_hbm, first_ref, count_ref,
    fo_ref, to_ref, fkg_ref, fvg_ref, tkg_ref, tvg_ref,
    frames, tx, win, bias, s_scr, a_scr, b_scr, p_scr, ec_scr, x_low, y_low, fd_scr,
    st, st_m1, st_p1, st_m2, st_p2, fac,
    uvs, uvr, uvo, tks, tkr, tko,
    tx_sem, fl_sem, xl_sem, xs_sem, xr_sem, us_sem, ur_sem, ds_sem, dr_sem,
    ss_sem, sr_sem, uvs_sem, uvr_sem, tks_sem, tkr_sem,
):
    f = lax.axis_index("frame")
    t = lax.axis_index("text")
    rows = tx.shape[1]
    n_frames = frames.shape[1]
    blocks = n_frames // BLOCK
    scale = 1.0 / math.sqrt(D)
    scale2 = scale * math.log2(math.e)
    up1, up2 = lax.rem(f + 1, fdim), lax.rem(f + 2, fdim)
    dn1, dn2 = lax.rem(f + fdim - 1, fdim), lax.rem(f + fdim - 2, fdim)
    own = pl.ds(pl.multiple_of(t * rows, rows), rows)
    has_up, has_up2 = f < fdim - 1, f < fdim - 2
    has_dn, has_dn2 = f > 0, f > 1

    def lanes(i):
        return pl.ds(pl.multiple_of(i * D, D), D)

    def tx_load(a):
        return pltpu.make_async_copy((tk_hbm, tv_hbm, tg_hbm)[a], tx.at[a], tx_sem.at[a])

    def frame_load(a):
        return pltpu.make_async_copy((fk_hbm, fv_hbm, fg_hbm)[a], frames.at[a], fl_sem.at[a])

    def remote(src, dst, send, recv, frame, text):
        return pltpu.make_async_remote_copy(
            src_ref=src, dst_ref=dst, send_sem=send, recv_sem=recv,
            device_id=(frame, text), device_id_type=MESH,
        )

    def x_copy(h, d):
        peer = lax.rem(t + d, tdim)
        return remote(
            tx.at[:, :, lanes(peer * heads + h)], win.at[h, :, 1, own, :],
            xs_sem, xr_sem.at[h, d - 1], f, peer,
        )

    def x_own(h):
        return pltpu.make_async_copy(
            tx.at[:, :, lanes(t * heads + h)], win.at[h, :, 1, own, :], xl_sem.at[h]
        )

    def piece(d):
        return pl.ds(pl.multiple_of(lax.rem(t + tdim - d, tdim) * rows, rows), rows)

    def window(h, d):
        if d is None:
            return (
                remote(win.at[h, :, 1], win.at[h, :, 0], us_sem, ur_sem.at[h], up1, t),
                remote(win.at[h, :, 1], win.at[h, :, 2], ds_sem, dr_sem.at[h], dn1, t),
            )
        at = piece(d)
        src = win.at[h, :, 1, at, :] if d else tx.at[:, :, lanes(t * heads + h)]
        return (
            remote(src, win.at[h, :, 0, at, :], us_sem, ur_sem.at[h], up1, t),
            remote(src, win.at[h, :, 2, at, :], ds_sem, dr_sem.at[h], dn1, t),
        )

    def stats(h):
        a, b = st.at[h, 0], st.at[h, 1]
        return (
            remote(a, st_m1.at[h], ss_sem.at[0], sr_sem.at[h, 0], up1, t),
            remote(b, st_p1.at[h], ss_sem.at[1], sr_sem.at[h, 1], dn1, t),
        )

    def stats2(h):
        a, b = st.at[h, 0], st.at[h, 1]
        return (
            remote(a, st_m2.at[h], ss_sem.at[2], sr_sem.at[h, 2], up2, t),
            remote(b, st_p2.at[h], ss_sem.at[3], sr_sem.at[h, 3], dn2, t),
        )

    def uv_copies(h):
        return (
            remote(uvs.at[h, 1], uvr.at[h, 1], uvs_sem.at[1], uvr_sem.at[h, 1], up1, t),
            remote(uvs.at[h, 0], uvr.at[h, 0], uvs_sem.at[0], uvr_sem.at[h, 0], dn1, t),
        )

    def tk_copies(h):
        return (
            remote(tks.at[h, 1], tkr.at[h, 1], tks_sem.at[1], tkr_sem.at[h, 1], up1, t),
            remote(tks.at[h, 0], tkr.at[h, 0], tks_sem.at[0], tkr_sem.at[h, 0], dn1, t),
        )

    def each(action, ups, downs, *pairs):
        @pl.when(ups)
        def _():
            for pair in pairs:
                getattr(pair[0], action)()

        @pl.when(downs)
        def _():
            for pair in pairs:
                getattr(pair[1], action)()

    def start(*pairs):
        each("start", has_up, has_dn, *pairs)

    def arrived(*pairs):
        each("wait_recv", has_dn, has_up, *pairs)

    def sent(*pairs):
        each("wait_send", has_up, has_dn, *pairs)

    for a in range(3):
        tx_load(a).start()

    barrier = pltpu.get_barrier_semaphore()
    for d in range(1, tdim):
        pl.semaphore_signal(
            barrier, inc=1, device_id=(f, lax.rem(t + d, tdim)), device_id_type=MESH
        )
    for there, frame in ((has_up, up1), (has_dn, dn1), (has_up2, up2), (has_dn2, dn2)):

        @pl.when(there)
        def _():
            pl.semaphore_signal(barrier, inc=1, device_id=(frame, t), device_id_type=MESH)

    for a in range(3):
        frame_load(a).start()

    def blank(tile):
        tile[...] = jnp.ones(tile.shape, F32)
        tile[:, 0:1, :] = jnp.full((heads, 1, BLOCK), FLOOR, F32)
        tile[:, 3:4, :] = jnp.full((heads, 1, BLOCK), FLOOR, F32)

    for there, slot, tile, side in ((has_dn, 0, st_m1, 1), (has_up, 2, st_p1, 0)):

        @pl.when(jnp.logical_not(there))
        def _():
            blank(tile)

            @pl.loop(0, heads)
            def _(h):
                for a in range(3):
                    win[h, a, slot] = jnp.zeros((BLOCK, D), BF16)
                for a in range(2):
                    uvr[h, side, a] = jnp.zeros((D, BLOCK), BF16)
                tkr[h, side] = jnp.zeros((D, BLOCK), BF16)

    for there, tile in ((has_dn2, st_m2), (has_up2, st_p2)):

        @pl.when(jnp.logical_not(there))
        def _():
            blank(tile)

    for b in range(blocks):
        for s in range(3):
            text_id = f - 1 + s
            low = first_ref[b]
            live = (text_id >= low) & (text_id < low + count_ref[b]) & (text_id < fdim)
            bias[b, :, s * BLOCK : (s + 1) * BLOCK] = jnp.full(
                (1, BLOCK), jnp.where(live, 0.0, NEGATIVE), F32
            )

    peers = sum(there.astype(jnp.int32) for there in (has_up, has_dn, has_up2, has_dn2))
    pl.semaphore_wait(barrier, peers + tdim - 1)

    for a in range(3):
        tx_load(a).wait()

    @pl.loop(0, heads)
    def _(h):
        for d in range(1, tdim):
            x_copy(h, d).start()
        start(window(h, 0))
        x_own(h).start()

    def forward(h):
        for d in range(1, tdim):
            x_copy(h, d).wait_recv()
            start(window(h, d))

    def text(h, a):
        return win[h, a].reshape(3 * BLOCK, D)

    def part(b):
        return slice(b * BLOCK, (b + 1) * BLOCK)

    def phase1(h):
        x_own(h).wait()
        arrived(window(h, None))
        s_scr[...] = dot_nt(frames[0, :, lanes(h)], text(h, 0))
        b_scr[h] = dot_nt(frames[1, :, lanes(h)], text(h, 2))
        peak = jnp.full((1, 3 * BLOCK), FLOOR, F32)
        for b in range(blocks):
            s = s_scr[part(b), :] * scale2 + bias[b]
            s_scr[part(b), :] = s
            peak = jnp.maximum(peak, jnp.max(s, axis=0, keepdims=True))
            e = jnp.exp2(s - jnp.max(s, axis=1, keepdims=True))
            p = e * (1.0 / jnp.sum(e, axis=1, keepdims=True))
            p_scr[h, part(b), :] = p
            x_low[part(b), :] = p.astype(BF16)
        total = jnp.zeros((1, 3 * BLOCK), F32)
        dots = jnp.zeros((1, 3 * BLOCK), F32)
        for b in range(blocks):
            e = jnp.exp2(s_scr[part(b), :] - peak)
            ec_scr[h, part(b), :] = e
            y_low[part(b), :] = e.astype(BF16)
            total = total + jnp.sum(e, axis=0, keepdims=True)
            dots = dots + jnp.sum(e * b_scr[h, part(b), :], axis=0, keepdims=True)
        for i, pair in enumerate(((1, 2), (0, 1))):
            for j, slot in enumerate(pair):
                for k, row in enumerate((peak, total, dots)):
                    st[h, i, 3 * j + k : 3 * j + k + 1, :] = row[:, part(slot)]
        start(stats(h))
        each("start", has_up2, has_dn2, stats2(h))
        u = dot_tn(frames[1, :, lanes(h)], y_low[...])
        v = dot_tn(frames[2, :, lanes(h)], x_low[...])
        for i, value in enumerate((u, v)):
            uvs[h, 0, i] = value[:, part(0)].astype(BF16)
            uvo[h, i] = value[:, part(1)]
            uvs[h, 1, i] = value[:, part(2)].astype(BF16)
        start(uv_copies(h))
        out = dot_nn(x_low[...], text(h, 1)).astype(BF16)
        fo_ref[:, lanes(h)] = out
        fd_scr[h] = jnp.sum(
            out.astype(F32) * frames[2, :, lanes(h)].astype(F32), axis=1, keepdims=True
        )

    def phase2(h):
        arrived(stats(h))
        each("wait_recv", has_dn2, has_up2, stats2(h))
        a, b, m1, p1, m2, p2 = st[h, 0], st[h, 1], st_m1[h], st_p1[h], st_m2[h], st_p2[h]
        members = (
            (b[0:3], m1[0:3], m2[3:6]),
            (a[0:3], m1[3:6], p1[0:3]),
            (a[3:6], p1[3:6], p2[0:3]),
        )
        gains, dots = [], []
        for s, tiles in enumerate(members):
            tops = [tile[0:1] for tile in tiles]
            peak = functools.reduce(jnp.maximum, tops)
            factors = [jnp.exp2(top - peak) for top in tops]
            total = sum(tile[1:2] * factor for tile, factor in zip(tiles, factors))
            inverse = 1.0 / total
            dot = sum(tile[2:3] * factor for tile, factor in zip(tiles, factors)) * inverse
            gains.append(factors[0] * inverse)
            dots.append(dot)
            if s == 1:
                for i in range(3):
                    fac[h, i : i + 1, :] = factors[i] * inverse
        gain = jnp.concatenate(gains, axis=1)
        text_dot = jnp.concatenate(dots, axis=1)
        a_scr[...] = dot_nt(frames[2, :, lanes(h)], text(h, 1))
        for b in range(blocks):
            c = ec_scr[h, part(b), :] * gain
            y_low[part(b), :] = c.astype(BF16)
            g = p_scr[h, part(b), :] * (a_scr[part(b), :] - fd_scr[h, part(b), :]) + c * (
                b_scr[h, part(b), :] - text_dot
            )
            x_low[part(b), :] = g.astype(BF16)
        k = dot_tn(frames[0, :, lanes(h)], x_low[...])
        tks[h, 0] = k[:, part(0)].astype(BF16)
        tko[h] = k[:, part(1)]
        tks[h, 1] = k[:, part(2)].astype(BF16)
        start(tk_copies(h))
        fkg_ref[:, lanes(h)] = (scale * dot_nn(x_low[...], text(h, 0))).astype(BF16)
        fvg_ref[:, lanes(h)] = dot_nn(y_low[...], text(h, 2)).astype(BF16)

    def phase3(h):
        arrived(uv_copies(h), tk_copies(h))
        out = (
            uvo[h, 0] * fac[h, 0:1, :]
            + uvr[h, 1, 0].astype(F32) * fac[h, 1:2, :]
            + uvr[h, 0, 0].astype(F32) * fac[h, 2:3, :]
        )
        to_ref[:, lanes(h)] = out.T.astype(BF16)
        keys = scale * (tko[h] + tkr[h, 1].astype(F32) + tkr[h, 0].astype(F32))
        tkg_ref[:, lanes(h)] = keys.T.astype(BF16)
        values = uvo[h, 1] + uvr[h, 1, 1].astype(F32) + uvr[h, 0, 1].astype(F32)
        tvg_ref[:, lanes(h)] = values.T.astype(BF16)

    ahead = min(AHEAD, heads)
    lag = min(LAG, heads)

    @pl.loop(0, ahead)
    def _(h):
        forward(h)

    for a in range(3):
        frame_load(a).wait()

    @pl.loop(0, heads + lag + 1)
    def _(i):
        @pl.when(i < heads)
        def _():
            phase1(i)

        @pl.when(i + ahead < heads)
        def _():
            forward(i + ahead)

        @pl.when((i >= lag) & (i < heads + lag))
        def _():
            phase2(i - lag)

        @pl.when(i >= lag + 1)
        def _():
            phase3(i - lag - 1)

    def total(ref, sem):
        return remote(ref, ref, sem, sem, up1, t)

    total(win.at[:, :, 1, pl.ds(0, (tdim - 1) * rows), :], xs_sem).wait_send()
    sent(
        (total(win.at[:, :, 0], us_sem), total(win.at[:, :, 2], ds_sem)),
        (total(st_m1, ss_sem.at[0]), total(st_p1, ss_sem.at[1])),
        (total(uvr.at[:, 1], uvs_sem.at[1]), total(uvr.at[:, 0], uvs_sem.at[0])),
        (total(tkr.at[:, 1], tks_sem.at[1]), total(tkr.at[:, 0], tks_sem.at[0])),
    )
    each(
        "wait_send", has_up2, has_dn2,
        (total(st_m2, ss_sem.at[2]), total(st_p2, ss_sem.at[3])),
    )


def writer(*refs):
    sources, targets, sem = refs[:6], refs[6:12], refs[12]
    copies = [
        pltpu.make_async_copy(sources[i], targets[i], sem.at[i]) for i in range(6)
    ]
    for copy in copies:
        copy.start()
    for copy in copies:
        copy.wait()


def on_device(fdim, tdim, *args):
    n_frames, width = args[0].shape
    rows = args[3].shape[0]
    heads = width // D
    own_rows = rows * tdim
    window = 3 * BLOCK
    blocks = n_frames // BLOCK
    shape = jax.ShapeDtypeStruct
    frame_out, text_out = shape((n_frames, width), BF16), shape((own_rows, width), BF16)
    dma = pltpu.SemaphoreType.DMA
    vmem = pltpu.VMEM
    hbm_spec = pl.BlockSpec(memory_space=pltpu.HBM)
    vmem_spec = pl.BlockSpec(memory_space=pltpu.VMEM)
    smem_spec = pl.BlockSpec(memory_space=pltpu.SMEM)
    outs = (frame_out, text_out, frame_out, frame_out, text_out, text_out)
    results = pl.pallas_call(
        functools.partial(kernel, fdim, tdim, heads),
        out_shape=tuple(vmem(out.shape, out.dtype) for out in outs),
        in_specs=[hbm_spec] * 6 + [smem_spec] * 2,
        out_specs=(vmem_spec,) * 6,
        scratch_shapes=[
            vmem((3, n_frames, width), BF16),
            vmem((3, rows, args[3].shape[1]), BF16),
            vmem((heads, 3, 3, BLOCK, D), BF16),
            vmem((blocks, 1, window), F32),
            vmem((n_frames, window), F32),
            vmem((n_frames, window), F32),
            vmem((heads, n_frames, window), F32),
            vmem((heads, n_frames, window), F32),
            vmem((heads, n_frames, window), F32),
            vmem((n_frames, window), BF16),
            vmem((n_frames, window), BF16),
            vmem((heads, n_frames, 1), F32),
            vmem((heads, 2, 8, BLOCK), F32),
            vmem((heads, 8, BLOCK), F32),
            vmem((heads, 8, BLOCK), F32),
            vmem((heads, 8, BLOCK), F32),
            vmem((heads, 8, BLOCK), F32),
            vmem((heads, 8, BLOCK), F32),
            vmem((heads, 2, 2, D, BLOCK), BF16),
            vmem((heads, 2, 2, D, BLOCK), BF16),
            vmem((heads, 2, D, BLOCK), F32),
            vmem((heads, 2, D, BLOCK), BF16),
            vmem((heads, 2, D, BLOCK), BF16),
            vmem((heads, D, BLOCK), F32),
            dma((3,)),
            dma((3,)),
            dma((heads,)),
            dma,
            dma((heads, max(tdim - 1, 1))),
            dma,
            dma((heads,)),
            dma,
            dma((heads,)),
            dma((4,)),
            dma((heads, 4)),
            dma((2,)),
            dma((heads, 2)),
            dma((2,)),
            dma((heads, 2)),
        ],
        compiler_params=pltpu.CompilerParams(
            collective_id=0, has_side_effects=True, vmem_limit_bytes=60 << 20
        ),
    )(*args)
    return pl.pallas_call(
        writer,
        out_shape=outs,
        in_specs=[vmem_spec] * 6,
        out_specs=(hbm_spec,) * 6,
        scratch_shapes=[dma((6,))],
        compiler_params=pltpu.CompilerParams(vmem_limit_bytes=1 << 20),
    )(*results)


def solution(mesh):
    whole = P("frame", "text")
    split = P(("frame", "text"), None)
    return jax.shard_map(
        functools.partial(on_device, mesh.shape["frame"], mesh.shape["text"]),
        mesh=mesh,
        in_specs=(whole,) * 3 + (split,) * 3 + (P("frame"),) * 2,
        out_specs=(whole,) * 6,
        check_vma=False,
    )
```

profile of v0, /device:TPU:24, one launch (start us, length us, event | category | flops | bytes accessed | tf_op | source)
XLA Modules:
  0.0 47.0 jit_solution(10611176046733517900)
XLA Ops:
  0.6 44.4 %shard_map.127 = (bf16[512,1024]{1,0:T(8,128)(2,1)S(1)}, bf16[128,1024]{1,0:T(8,128)(2,1)S(1)}, bf16[512,1024]{1,0:T(8,128)(2,1)S(1)}, bf16[512,1024]{1,0:T(8,12...) custom-call(bf16[512,1024]{1,0:T(8,128)(2,1)} %fk_hbm.1, bf16[512,1024]{1,0:T(8,128)(2,1)} %fv_hbm.1, ...), custom_call_target="tpu_custom_call" | custom-call | tf_op jit(solution)/shard_map/pallas_call | solution.py:385
  45.1 2.0 %shard_map.128 = (bf16[512,1024]{1,0:T(8,128)(2,1)}, bf16[128,1024]{1,0:T(8,128)(2,1)}, bf16[512,1024]{1,0:T(8,128)(2,1)}, bf16[512,1024]{1,0:T(8,128)(2,1)}, bf...) custom-call(bf16[512,1024]{1,0:T(8,128)(2,1)S(1)} %get-tuple-element.12.refs_0_, ...), custom_call_target="tpu_custom_call" | custom-call | tf_op jit(solution)/shard_map/pallas_call | solution.py:435
where the time goes:
time: 47.1 us; the launch traced here: 47 us
  Pallas kernels  46.4 us (99%)
  between operations  0.64 us (1%)
    pallas_call x1, Pallas kernels, on_device(): pl.pallas_call(functools.partial(kernel, fdim, tdim, heads), out_shape=tu...  44.4 us
    pallas_call x1, Pallas kernels, on_device(): pl.pallas_call(writer, out_shape=outs, in_specs=[vmem_spec] * 6, out_spec...  1.97 us

commit v1 on v0

--- a/solution.py
+++ b/solution.py
@@ -12,8 +12,10 @@
 BLOCK = 128
 NEGATIVE = -1e30
 FLOOR = -1e20
-LAG = 2
-AHEAD = 4
+LAG = 3
+FIRST = 3
+HOLD = 5
+BULK = 3
 MESH = pl.DeviceIdType.MESH
 F32 = jnp.float32
 BF16 = jnp.bfloat16
@@ -35,7 +37,8 @@
     fdim, tdim, heads,
     fk_hbm, fv_hbm, fg_hbm, tk_hbm, tv_hbm, tg_hbm, first_ref, count_ref,
     fo_ref, to_ref, fkg_ref, fvg_ref, tkg_ref, tvg_ref,
-    frames, tx, win, bias, s_scr, a_scr, b_scr, p_scr, ec_scr, x_low, y_low, fd_scr,
+    frames, tx, win, bias, s_scr, a_scr, b_scr, p_scr, ec_scr,
+    xs_low, ys_low, gs_low, cs_low, turned, fd_scr,
     st, st_m1, st_p1, st_m2, st_p2, fac,
     uvs, uvr, uvo, tks, tkr, tko,
     tx_sem, fl_sem, xl_sem, xs_sem, xr_sem, us_sem, ur_sem, ds_sem, dr_sem,
@@ -55,6 +58,8 @@
     has_dn, has_dn2 = f > 0, f > 1
 
     def lanes(i):
+        if isinstance(i, int):
+            return slice(i * D, (i + 1) * D)
         return pl.ds(pl.multiple_of(i * D, D), D)
 
     def tx_load(a):
@@ -123,25 +128,34 @@
             remote(tks.at[h, 0], tkr.at[h, 0], tks_sem.at[0], tkr_sem.at[h, 0], dn1, t),
         )
 
-    def each(action, ups, downs, *pairs):
-        @pl.when(ups)
-        def _():
-            for pair in pairs:
-                getattr(pair[0], action)()
-
-        @pl.when(downs)
-        def _():
-            for pair in pairs:
-                getattr(pair[1], action)()
-
-    def start(*pairs):
-        each("start", has_up, has_dn, *pairs)
-
-    def arrived(*pairs):
-        each("wait_recv", has_dn, has_up, *pairs)
-
-    def sent(*pairs):
-        each("wait_send", has_up, has_dn, *pairs)
+    def act(action, *guarded):
+        for there, copies in guarded:
+
+            @pl.when(there)
+            def _():
+                for copy in copies:
+                    getattr(copy, action)()
+
+    def split(pairs):
+        return [pair[0] for pair in pairs], [pair[1] for pair in pairs]
+
+    def start(pairs, far=()):
+        if not pairs:
+            return
+        ups, downs = split(pairs)
+        act("start", (has_up, ups), (has_dn, downs))
+        if far:
+            ups, downs = split(far)
+            act("start", (has_up2, ups), (has_dn2, downs))
+
+    def arrived(pairs, far=()):
+        if not pairs:
+            return
+        ups, downs = split(pairs)
+        act("wait_recv", (has_dn, ups), (has_up, downs))
+        if far:
+            ups, downs = split(far)
+            act("wait_recv", (has_dn2, ups), (has_up2, downs))
 
     for a in range(3):
         tx_load(a).start()
@@ -204,13 +218,13 @@
     def _(h):
         for d in range(1, tdim):
             x_copy(h, d).start()
-        start(window(h, 0))
+        start([window(h, 0)])
         x_own(h).start()
 
     def forward(h):
         for d in range(1, tdim):
             x_copy(h, d).wait_recv()
-            start(window(h, d))
+        start([window(h, d) for d in range(1, tdim)])
 
     def text(h, a):
         return win[h, a].reshape(3 * BLOCK, D)
@@ -218,9 +232,8 @@
     def part(b):
         return slice(b * BLOCK, (b + 1) * BLOCK)
 
-    def phase1(h):
-        x_own(h).wait()
-        arrived(window(h, None))
+    def softmax(h):
+        x_low, y_low = xs_low.at[h % 2], ys_low.at[h % 2]
         s_scr[...] = dot_nt(frames[0, :, lanes(h)], text(h, 0))
         b_scr[h] = dot_nt(frames[1, :, lanes(h)], text(h, 2))
         peak = jnp.full((1, 3 * BLOCK), FLOOR, F32)
@@ -244,24 +257,23 @@
             for j, slot in enumerate(pair):
                 for k, row in enumerate((peak, total, dots)):
                     st[h, i, 3 * j + k : 3 * j + k + 1, :] = row[:, part(slot)]
-        start(stats(h))
-        each("start", has_up2, has_dn2, stats2(h))
-        u = dot_tn(frames[1, :, lanes(h)], y_low[...])
-        v = dot_tn(frames[2, :, lanes(h)], x_low[...])
+
+    def values(h):
+        x_low, y_low = xs_low.at[h % 2], ys_low.at[h % 2]
+        u = dot_nn(turned[1, h], y_low[...])
+        v = dot_nn(turned[2, h], x_low[...])
         for i, value in enumerate((u, v)):
             uvs[h, 0, i] = value[:, part(0)].astype(BF16)
             uvo[h, i] = value[:, part(1)]
             uvs[h, 1, i] = value[:, part(2)].astype(BF16)
-        start(uv_copies(h))
         out = dot_nn(x_low[...], text(h, 1)).astype(BF16)
         fo_ref[:, lanes(h)] = out
         fd_scr[h] = jnp.sum(
             out.astype(F32) * frames[2, :, lanes(h)].astype(F32), axis=1, keepdims=True
         )
 
-    def phase2(h):
-        arrived(stats(h))
-        each("wait_recv", has_dn2, has_up2, stats2(h))
+    def scores_grad(h):
+        g_low, c_low = gs_low.at[h % 2], cs_low.at[h % 2]
         a, b, m1, p1, m2, p2 = st[h, 0], st[h, 1], st_m1[h], st_p1[h], st_m2[h], st_p2[h]
         members = (
             (b[0:3], m1[0:3], m2[3:6]),
@@ -286,21 +298,22 @@
         a_scr[...] = dot_nt(frames[2, :, lanes(h)], text(h, 1))
         for b in range(blocks):
             c = ec_scr[h, part(b), :] * gain
-            y_low[part(b), :] = c.astype(BF16)
+            c_low[part(b), :] = c.astype(BF16)
             g = p_scr[h, part(b), :] * (a_scr[part(b), :] - fd_scr[h, part(b), :]) + c * (
                 b_scr[h, part(b), :] - text_dot
             )
-            x_low[part(b), :] = g.astype(BF16)
-        k = dot_tn(frames[0, :, lanes(h)], x_low[...])
+            g_low[part(b), :] = g.astype(BF16)
+
+    def grads(h):
+        g_low, c_low = gs_low.at[h % 2], cs_low.at[h % 2]
+        k = dot_nn(turned[0, h], g_low[...])
         tks[h, 0] = k[:, part(0)].astype(BF16)
         tko[h] = k[:, part(1)]
         tks[h, 1] = k[:, part(2)].astype(BF16)
-        start(tk_copies(h))
-        fkg_ref[:, lanes(h)] = (scale * dot_nn(x_low[...], text(h, 0))).astype(BF16)
-        fvg_ref[:, lanes(h)] = dot_nn(y_low[...], text(h, 2)).astype(BF16)
-
-    def phase3(h):
-        arrived(uv_copies(h), tk_copies(h))
+        fkg_ref[:, lanes(h)] = (scale * dot_nn(g_low[...], text(h, 0))).astype(BF16)
+        fvg_ref[:, lanes(h)] = dot_nn(c_low[...], text(h, 2)).astype(BF16)
+
+    def combine(h):
         out = (
             uvo[h, 0] * fac[h, 0:1, :]
             + uvr[h, 1, 0].astype(F32) * fac[h, 1:2, :]
@@ -312,47 +325,89 @@
         values = uvo[h, 1] + uvr[h, 1, 1].astype(F32) + uvr[h, 0, 1].astype(F32)
         tvg_ref[:, lanes(h)] = values.T.astype(BF16)
 
-    ahead = min(AHEAD, heads)
-    lag = min(LAG, heads)
-
-    @pl.loop(0, ahead)
-    def _(h):
-        forward(h)
-
     for a in range(3):
         frame_load(a).wait()
 
-    @pl.loop(0, heads + lag + 1)
-    def _(i):
-        @pl.when(i < heads)
-        def _():
-            phase1(i)
-
-        @pl.when(i + ahead < heads)
-        def _():
-            forward(i + ahead)
-
-        @pl.when((i >= lag) & (i < heads + lag))
-        def _():
-            phase2(i - lag)
-
-        @pl.when(i >= lag + 1)
-        def _():
-            phase3(i - lag - 1)
+    @pl.loop(0, heads)
+    def _(h):
+        for a in range(3):
+            turned[a, h] = frames[a, :, lanes(h)].T
+
+    first = min(FIRST, heads)
+    for h in range(first):
+        forward(h)
+
+    def within(h, stop=heads):
+        return [h] if 0 <= h < stop else []
+
+    sends, pending, i = [], [], 0
+    while i < heads + LAG + 1 or pending:
+        pending += [(uv_copies, h) for h in within(i - 1)]
+        pending += [(tk_copies, h) for h in within(i - LAG - 1, heads - 1)]
+        pending += [(tk_copies, h) for h in within(i - LAG) if h == heads - 1]
+        count = 0 if i < HOLD else BULK if i < heads else len(pending)
+        sends.append(pending[:count])
+        pending = pending[count:]
+        i += 1
+    def body(i):
+        now, after, middle = within(i), within(i - 1), within(i - LAG)
+        late = within(i - LAG - 1, heads - 1)
+        last = [h for h in middle if h == heads - 1]
+        for h in now:
+            x_own(h).wait()
+        arrived(
+            [window(h, None) for h in now] + [stats(h) for h in middle],
+            [stats2(h) for h in middle],
+        )
+        for h in late:
+            grads(h)
+        for h in middle:
+            scores_grad(h)
+        for h in now:
+            softmax(h)
+        for h in after:
+            values(h)
+        for h in last:
+            grads(h)
+        bulk = sends[i]
+        start([stats(h) for h in now] + [c(h) for c, h in bulk], [stats2(h) for h in now])
+        if i + first < heads:
+            forward(i + first)
+
+    for i in range(len(sends)):
+        body(i)
+
+    @pl.loop(0, heads)
+    def _(h):
+        arrived([uv_copies(h), tk_copies(h)])
+        combine(h)
 
     def total(ref, sem):
         return remote(ref, ref, sem, sem, up1, t)
 
     total(win.at[:, :, 1, pl.ds(0, (tdim - 1) * rows), :], xs_sem).wait_send()
-    sent(
-        (total(win.at[:, :, 0], us_sem), total(win.at[:, :, 2], ds_sem)),
-        (total(st_m1, ss_sem.at[0]), total(st_p1, ss_sem.at[1])),
-        (total(uvr.at[:, 1], uvs_sem.at[1]), total(uvr.at[:, 0], uvs_sem.at[0])),
-        (total(tkr.at[:, 1], tks_sem.at[1]), total(tkr.at[:, 0], tks_sem.at[0])),
-    )
-    each(
-        "wait_send", has_up2, has_dn2,
-        (total(st_m2, ss_sem.at[2]), total(st_p2, ss_sem.at[3])),
+    act(
+        "wait_send",
+        (
+            has_up,
+            [
+                total(win.at[:, :, 0], us_sem),
+                total(st_m1, ss_sem.at[0]),
+                total(uvr.at[:, 1], uvs_sem.at[1]),
+                total(tkr.at[:, 1], tks_sem.at[1]),
+            ],
+        ),
+        (
+            has_dn,
+            [
+                total(win.at[:, :, 2], ds_sem),
+                total(st_p1, ss_sem.at[1]),
+                total(uvr.at[:, 0], uvs_sem.at[0]),
+                total(tkr.at[:, 0], tks_sem.at[0]),
+            ],
+        ),
+        (has_up2, [total(st_m2, ss_sem.at[2])]),
+        (has_dn2, [total(st_p2, ss_sem.at[3])]),
     )
 
 
@@ -397,8 +452,11 @@
             vmem((heads, n_frames, window), F32),
             vmem((heads, n_frames, window), F32),
             vmem((heads, n_frames, window), F32),
-            vmem((n_frames, window), BF16),
-            vmem((n_frames, window), BF16),
+            vmem((2, n_frames, window), BF16),
+            vmem((2, n_frames, window), BF16),
+            vmem((2, n_frames, window), BF16),
+            vmem((2, n_frames, window), BF16),
+            vmem((3, heads, D, n_frames), BF16),
             vmem((heads, n_frames, 1), F32),
             vmem((heads, 2, 8, BLOCK), F32),
             vmem((heads, 8, BLOCK), F32),

time: 47.1 us -> 42.1 us (0.89)
  Pallas kernels: 46.4 us -> 41.3 us
    pallas_call x1, Pallas kernels: 44.4 us -> 39.4 us  [on_device(): pl.pallas_call(functools.partial(kernel, fdim, tdim, heads), out_shape=tu...]
where the time goes in v1:
time: 42.1 us; the launch traced here: 42 us
  Pallas kernels  41.3 us (98%)
  between operations  0.64 us (2%)
    pallas_call x1, Pallas kernels, on_device(): pl.pallas_call(functools.partial(kernel, fdim, tdim, heads), out_shape=tu...  39.4 us
    pallas_call x1, Pallas kernels, on_device(): pl.pallas_call(writer, out_shape=outs, in_specs=[vmem_spec] * 6, out_spec...  1.97 us

profile of v1, /device:TPU:24, one launch (start us, length us, event | category | flops | bytes accessed | tf_op | source)
XLA Modules:
  0.0 42.0 jit_solution(1312480753085780433)
XLA Ops:
  0.6 39.4 %shard_map.127 = (bf16[512,1024]{1,0:T(8,128)(2,1)S(1)}, bf16[128,1024]{1,0:T(8,128)(2,1)S(1)}, bf16[512,1024]{1,0:T(8,128)(2,1)S(1)}, bf16[512,1024]{1,0:T(8,12...) custom-call(bf16[512,1024]{1,0:T(8,128)(2,1)} %fk_hbm.1, bf16[512,1024]{1,0:T(8,128)(2,1)} %fv_hbm.1, ...), custom_call_target="tpu_custom_call" | custom-call | tf_op jit(solution)/shard_map/pallas_call | solution.py:440
  40.0 2.0 %shard_map.128 = (bf16[512,1024]{1,0:T(8,128)(2,1)}, bf16[128,1024]{1,0:T(8,128)(2,1)}, bf16[512,1024]{1,0:T(8,128)(2,1)}, bf16[512,1024]{1,0:T(8,128)(2,1)}, bf...) custom-call(bf16[512,1024]{1,0:T(8,128)(2,1)S(1)} %get-tuple-element.12.refs_0_, ...), custom_call_target="tpu_custom_call" | custom-call | tf_op jit(solution)/shard_map/pallas_call | solution.py:493

commit v2 on v1

--- a/solution.py
+++ b/solution.py
@@ -12,8 +12,8 @@
 BLOCK = 128
 NEGATIVE = -1e30
 FLOOR = -1e20
-LAG = 3
-FIRST = 3
+LAG = 4
+FIRST = 5
 HOLD = 5
 BULK = 3
 MESH = pl.DeviceIdType.MESH

time: 42.1 us -> 40.2 us (0.955)
  Pallas kernels: 41.3 us -> 39.1 us
    pallas_call x1, Pallas kernels: 39.4 us -> 37.1 us  [on_device(): pl.pallas_call(functools.partial(kernel, fdim, tdim, heads), out_shape=tu...]
where the time goes in v2:
time: 40.2 us; the launch traced here: 39.7 us
  Pallas kernels  39.1 us (97%)
  between operations  0.64 us (2%)
    pallas_call x1, Pallas kernels, on_device(): pl.pallas_call(functools.partial(kernel, fdim, tdim, heads), out_shape=tu...  37.1 us
    pallas_call x1, Pallas kernels, on_device(): pl.pallas_call(writer, out_shape=outs, in_specs=[vmem_spec] * 6, out_spec...  1.97 us

profile of v2, /device:TPU:24, one launch (start us, length us, event | category | flops | bytes accessed | tf_op | source)
XLA Modules:
  0.0 39.7 jit_solution(6546773213587077860)
XLA Ops:
  0.6 37.1 %shard_map.127 = (bf16[512,1024]{1,0:T(8,128)(2,1)S(1)}, bf16[128,1024]{1,0:T(8,128)(2,1)S(1)}, bf16[512,1024]{1,0:T(8,128)(2,1)S(1)}, bf16[512,1024]{1,0:T(8,12...) custom-call(bf16[512,1024]{1,0:T(8,128)(2,1)} %fk_hbm.1, bf16[512,1024]{1,0:T(8,128)(2,1)} %fv_hbm.1, ...), custom_call_target="tpu_custom_call" | custom-call | tf_op jit(solution)/shard_map/pallas_call | solution.py:440
  37.8 2.0 %shard_map.128 = (bf16[512,1024]{1,0:T(8,128)(2,1)}, bf16[128,1024]{1,0:T(8,128)(2,1)}, bf16[512,1024]{1,0:T(8,128)(2,1)}, bf16[512,1024]{1,0:T(8,128)(2,1)}, bf...) custom-call(bf16[512,1024]{1,0:T(8,128)(2,1)S(1)} %get-tuple-element.12.refs_0_, ...), custom_call_target="tpu_custom_call" | custom-call | tf_op jit(solution)/shard_map/pallas_call | solution.py:493

commit v3 on v2

--- a/solution.py
+++ b/solution.py
@@ -13,7 +13,7 @@
 NEGATIVE = -1e30
 FLOOR = -1e20
 LAG = 4
-FIRST = 5
+FIRST = 6
 HOLD = 5
 BULK = 3
 MESH = pl.DeviceIdType.MESH

time: 40.2 us -> 41.1 us (1.022)
  the two profiles are of different devices: /device:TPU:24 before, /device:TPU:1 now
where the time goes in v3:
time: 41.1 us; the launch traced here: 41 us
  Pallas kernels  40.4 us (98%)
  between operations  0.64 us (2%)
    pallas_call x1, Pallas kernels, on_device(): pl.pallas_call(functools.partial(kernel, fdim, tdim, heads), out_shape=tu...  38.4 us
    pallas_call x1, Pallas kernels, on_device(): pl.pallas_call(writer, out_shape=outs, in_specs=[vmem_spec] * 6, out_spec...  1.97 us

profile of v3, /device:TPU:1, one launch (start us, length us, event | category | flops | bytes accessed | tf_op | source)
XLA Modules:
  0.0 41.0 jit_solution(13094250282026028581)
XLA Ops:
  0.6 38.4 %shard_map.127 = (bf16[512,1024]{1,0:T(8,128)(2,1)S(1)}, bf16[128,1024]{1,0:T(8,128)(2,1)S(1)}, bf16[512,1024]{1,0:T(8,128)(2,1)S(1)}, bf16[512,1024]{1,0:T(8,12...) custom-call(bf16[512,1024]{1,0:T(8,128)(2,1)} %fk_hbm.1, bf16[512,1024]{1,0:T(8,128)(2,1)} %fv_hbm.1, ...), custom_call_target="tpu_custom_call" | custom-call | tf_op jit(solution)/shard_map/pallas_call | solution.py:440
  39.1 2.0 %shard_map.128 = (bf16[512,1024]{1,0:T(8,128)(2,1)}, bf16[128,1024]{1,0:T(8,128)(2,1)}, bf16[512,1024]{1,0:T(8,128)(2,1)}, bf16[512,1024]{1,0:T(8,128)(2,1)}, bf...) custom-call(bf16[512,1024]{1,0:T(8,128)(2,1)S(1)} %get-tuple-element.12.refs_0_, ...), custom_call_target="tpu_custom_call" | custom-call | tf_op jit(solution)/shard_map/pallas_call | solution.py:493
